TPU v7x, 32 devices: a whole 2x2x4 slice. The times are simulated.
32 devices in a mesh: group: 8 (over y, x, core), replica: 4 (over z).
Axes of the slice: x: 2, y: 2, z: 4, core: 2. Of those that a mesh axis runs over, the one named last changes fastest.
Arguments:
- inputs: bfloat16 [64, 512, 768], P(('group', 'replica')), may hold values from -6 to 6
- cotangent: bfloat16 [64, 512, 768], P(('group', 'replica')), may hold values from -6 to 6
- lengths: int32 [64], P(('group', 'replica')), may hold values from 128 to 512, as said below
- query_weight: bfloat16 [768, 768], P('group'), may hold values from -0.21875 to 0.21875
- key_weight: bfloat16 [768, 768], P('group'), may hold values from -0.21875 to 0.21875
- value_weight: bfloat16 [768, 768], P('group'), may hold values from -0.21875 to 0.21875
- out_weight: bfloat16 [768, 768], P('group'), may hold values from -3.5 to 3.5
- in_weight: bfloat16 [768, 3072], P('group'), may hold values from -0.21875 to 0.21875
- back_weight: bfloat16 [3072, 768], P('group'), may hold values from -0.109375 to 0.109375
- query_bias: bfloat16 [768], P('group'), may hold values from -1.796875 to 1.796875
- value_bias: bfloat16 [768], P('group'), may hold values from -1.796875 to 1.796875
- out_bias: bfloat16 [768], P('group'), may hold values from -1.796875 to 1.796875
- in_bias: bfloat16 [3072], P('group'), may hold values from -1.796875 to 1.796875
- back_bias: bfloat16 [768], P('group'), may hold values from -1.796875 to 1.796875
- first_gain: bfloat16 [768], P('group'), may hold values from 0.5 to 1.5
- first_shift: bfloat16 [768], P('group'), may hold values from -1.796875 to 1.796875
- second_gain: bfloat16 [768], P('group'), may hold values from 0.5 to 1.5
- second_shift: bfloat16 [768], P('group'), may hold values from -1.796875 to 1.796875
Outputs:
- layer_out: bfloat16 [64, 512, 768], P(('group', 'replica'))
- input_grad: bfloat16 [64, 512, 768], P(('group', 'replica'))
- query_weight_grad: float32 [768, 768], P('group')
- key_weight_grad: float32 [768, 768], P('group')
- value_weight_grad: float32 [768, 768], P('group')
- out_weight_grad: float32 [768, 768], P('group')
- in_weight_grad: float32 [768, 3072], P('group')
- back_weight_grad: float32 [3072, 768], P('group')
- query_bias_grad: float32 [768], P('group')
- value_bias_grad: float32 [768], P('group')
- out_bias_grad: float32 [768], P('group')
- in_bias_grad: float32 [3072], P('group')
- back_bias_grad: float32 [768], P('group')
- first_gain_grad: float32 [768], P('group')
- first_shift_grad: float32 [768], P('group')
- second_gain_grad: float32 [768], P('group')
- second_shift_grad: float32 [768], P('group')
Inputs may be any that keep to these rules, and one draw needn't show every extreme that they name: `lengths`: each sequence's valid tokens fill its first slots; some sequence has all 512 slots valid.
All inputs are finite; a program needn't handle non-finite values.
Results may differ from a plain program's by a relative error of at most 0.02.
Values may be sent and summed in bfloat16 or wider, within the bound.
No kernel may reach another device: no remote copies, remote signals or barrier semaphores. Data moves between devices by JAX's collectives and lax.ppermute only.
A program may use at most 192 MiB of HBM per device.

v0:
```python
import math
import jax
import jax.numpy as jnp
from jax import lax
from jax.sharding import PartitionSpec as P

HEADS = 12
HEAD_DIM = 64
NORM_EPS = 1e-12
inverse_root_two = 0.7071067811865476
inverse_root_tau = 0.3989422804014327


def for_sending(array):
    return jax.tree.map(lambda a: a.astype(jnp.bfloat16) if a.dtype == jnp.float32 else a, array)


def project(left, right):
    return jnp.dot(left, right, preferred_element_type=jnp.float32)


def outer_sum(left, right):
    return jnp.einsum("rd,re->de", left, right, preferred_element_type=jnp.float32)


def back_project(grad_rows, weight_full):
    return jnp.einsum("re,de->rd", grad_rows, weight_full, preferred_element_type=jnp.float32)


def norm_forward(hidden, norm_gain, norm_shift):
    centre = hidden - jnp.mean(hidden, -1, keepdims=True)
    inverse = lax.rsqrt(jnp.mean(centre * centre, -1, keepdims=True) + NORM_EPS)
    normed = centre * inverse
    return (normed * norm_gain + norm_shift, normed, inverse)


def norm_backward(grad_out, norm_gain, normed, inverse):
    scaled = grad_out * norm_gain
    centred = (
        scaled
        - jnp.mean(scaled, -1, keepdims=True)
        - normed * jnp.mean(scaled * normed, -1, keepdims=True)
    )
    return (inverse * centred, jnp.sum(grad_out * normed, 0), jnp.sum(grad_out, 0))


def gelu_slope(hidden):
    normal_cdf = 0.5 * (1.0 + lax.erf(hidden * inverse_root_two))
    density = jnp.exp(-0.5 * hidden * hidden) * inverse_root_tau
    return normal_cdf + hidden * density


def per_device(
    inputs,
    cotangent,
    lengths,
    query_weight,
    key_weight,
    value_weight,
    out_weight,
    in_weight,
    back_weight,
    query_bias,
    value_bias,
    out_bias,
    in_bias,
    back_bias,
    first_gain,
    first_shift,
    second_gain,
    second_shift,
):
    whole = (
        lax.all_gather(query_weight, "group", axis=0, tiled=True),
        lax.all_gather(key_weight, "group", axis=0, tiled=True),
        lax.all_gather(value_weight, "group", axis=0, tiled=True),
        lax.all_gather(out_weight, "group", axis=0, tiled=True),
        lax.all_gather(in_weight, "group", axis=0, tiled=True),
        lax.all_gather(back_weight, "group", axis=0, tiled=True),
        lax.all_gather(query_bias, "group", axis=0, tiled=True),
        lax.all_gather(value_bias, "group", axis=0, tiled=True),
        lax.all_gather(out_bias, "group", axis=0, tiled=True),
        lax.all_gather(in_bias, "group", axis=0, tiled=True),
        lax.all_gather(back_bias, "group", axis=0, tiled=True),
        lax.all_gather(first_gain, "group", axis=0, tiled=True),
        lax.all_gather(first_shift, "group", axis=0, tiled=True),
        lax.all_gather(second_gain, "group", axis=0, tiled=True),
        lax.all_gather(second_shift, "group", axis=0, tiled=True),
    )
    (
        full_query,
        full_key,
        full_value,
        full_out,
        full_in,
        full_back,
        bias_query,
        bias_value,
        bias_out,
        bias_in,
        bias_back,
        gain_first,
        shift_first,
        gain_second,
        shift_second,
    ) = whole
    seq_count, slot_count, model_width = inputs.shape
    total_rows = seq_count * slot_count
    block_rows = min(512, slot_count)
    seq_blocks = slot_count // block_rows
    item_count = seq_count * seq_blocks
    score_scale = 1.0 / math.sqrt(HEAD_DIM)
    flat_rows = inputs.reshape(total_rows, model_width)
    positions = lax.broadcasted_iota(jnp.int32, (seq_count, slot_count), 1)
    key_valid = positions < lengths[:, None]
    row_valid = key_valid.reshape(total_rows, 1).astype(jnp.float32)
    queries = (project(flat_rows, full_query) + bias_query.astype(jnp.float32)).astype(jnp.bfloat16)
    key_rows = project(flat_rows, full_key).astype(jnp.bfloat16)
    value_rows = (project(flat_rows, full_value) + bias_value.astype(jnp.float32)).astype(
        jnp.bfloat16
    )
    query_blocks = queries.reshape(item_count, block_rows, HEADS, HEAD_DIM)
    key_seqs = key_rows.reshape(seq_count, slot_count, HEADS, HEAD_DIM)
    value_seqs = value_rows.reshape(seq_count, slot_count, HEADS, HEAD_DIM)
    item_ids = jnp.arange(item_count, dtype=jnp.int32)

    def select_seq(item_id):
        seq_id = item_id // seq_blocks
        return (
            lax.dynamic_index_in_dim(key_seqs, seq_id, 0, False),
            lax.dynamic_index_in_dim(value_seqs, seq_id, 0, False),
            lax.dynamic_index_in_dim(key_valid, seq_id, 0, False),
        )

    def block_scores(query_part, key_part, valid_part):
        scores = (
            jnp.einsum("qhd,khd->hqk", query_part, key_part, preferred_element_type=jnp.float32)
            * score_scale
        )
        return jnp.where(valid_part[None, None, :], scores, -1e30)

    def attend(packed):
        query_part, item_id = packed
        key_part, value_part, valid_part = select_seq(item_id)
        scores = block_scores(query_part, key_part, valid_part)
        row_peak = jnp.max(scores, -1, keepdims=True)
        lifted = jnp.exp(scores - row_peak)
        normalizer = jnp.sum(lifted, -1, keepdims=True)
        soft_weights = (lifted / normalizer).astype(jnp.bfloat16)
        mixed_heads = jnp.einsum(
            "hqk,khd->qhd", soft_weights, value_part, preferred_element_type=jnp.float32
        )
        return (mixed_heads.astype(jnp.bfloat16), (row_peak + jnp.log(normalizer))[:, :, 0])

    mixed_blocks, log_sums = lax.map(attend, (query_blocks, item_ids))
    mixed_rows = mixed_blocks.reshape(total_rows, model_width)
    branch = project(mixed_rows, full_out) + bias_out.astype(jnp.float32)
    after_attn, normed_first, inverse_first = norm_forward(
        flat_rows.astype(jnp.float32) + branch,
        gain_first.astype(jnp.float32),
        shift_first.astype(jnp.float32),
    )
    after_low = after_attn.astype(jnp.bfloat16)
    hidden = project(after_low, full_in) + bias_in.astype(jnp.float32)
    active = jax.nn.gelu(hidden, approximate=False).astype(jnp.bfloat16)
    ffn_out = project(active, full_back) + bias_back.astype(jnp.float32)
    result_rows, normed_second, inverse_second = norm_forward(
        after_attn + ffn_out, gain_second.astype(jnp.float32), shift_second.astype(jnp.float32)
    )
    layer_out = result_rows.astype(jnp.bfloat16).reshape(seq_count, slot_count, model_width)
    again = (
        lax.all_gather(query_weight, "group", axis=0, tiled=True),
        lax.all_gather(key_weight, "group", axis=0, tiled=True),
        lax.all_gather(value_weight, "group", axis=0, tiled=True),
        lax.all_gather(out_weight, "group", axis=0, tiled=True),
        lax.all_gather(in_weight, "group", axis=0, tiled=True),
        lax.all_gather(back_weight, "group", axis=0, tiled=True),
        lax.all_gather(query_bias, "group", axis=0, tiled=True),
        lax.all_gather(value_bias, "group", axis=0, tiled=True),
        lax.all_gather(out_bias, "group", axis=0, tiled=True),
        lax.all_gather(in_bias, "group", axis=0, tiled=True),
        lax.all_gather(back_bias, "group", axis=0, tiled=True),
        lax.all_gather(first_gain, "group", axis=0, tiled=True),
        lax.all_gather(first_shift, "group", axis=0, tiled=True),
        lax.all_gather(second_gain, "group", axis=0, tiled=True),
        lax.all_gather(second_shift, "group", axis=0, tiled=True),
    )
    (
        back_query,
        back_key,
        back_value,
        back_out,
        back_in,
        back_ffn,
        unused_one,
        unused_two,
        unused_three,
        unused_four,
        unused_five,
        gain_first_b,
        unused_six,
        gain_second_b,
        unused_seven,
    ) = again
    grad_result = cotangent.reshape(total_rows, model_width).astype(jnp.float32) * row_valid
    grad_h2, second_gain_grad, second_shift_grad = norm_backward(
        grad_result, gain_second_b.astype(jnp.float32), normed_second, inverse_second
    )
    grad_ffn = grad_h2.astype(jnp.bfloat16)
    back_bias_grad = jnp.sum(grad_ffn.astype(jnp.float32), 0)
    back_weight_grad = outer_sum(active, grad_ffn)
    grad_hidden = (back_project(grad_ffn, back_ffn) * gelu_slope(hidden)).astype(jnp.bfloat16)
    in_bias_grad = jnp.sum(grad_hidden.astype(jnp.float32), 0)
    in_weight_grad = outer_sum(after_low, grad_hidden)
    grad_after = back_project(grad_hidden, back_in) + grad_h2
    grad_h1, first_gain_grad, first_shift_grad = norm_backward(
        grad_after, gain_first_b.astype(jnp.float32), normed_first, inverse_first
    )
    grad_branch = grad_h1.astype(jnp.bfloat16)
    out_bias_grad = jnp.sum(grad_branch.astype(jnp.float32), 0)
    out_weight_grad = outer_sum(mixed_rows, grad_branch)
    grad_mixed = back_project(grad_branch, back_out).astype(jnp.bfloat16)

    def attend_back(packed):
        query_part, grad_part, lse_part, item_id = packed
        key_part, value_part, valid_part = select_seq(item_id)
        scores = block_scores(query_part, key_part, valid_part)
        soft_weights = jnp.exp(scores - lse_part[:, :, None])
        grad_weights = jnp.einsum(
            "qhd,khd->hqk", grad_part, value_part, preferred_element_type=jnp.float32
        )
        grad_values = jnp.einsum(
            "hqk,qhd->khd",
            soft_weights.astype(jnp.bfloat16),
            grad_part,
            preferred_element_type=jnp.float32,
        )
        row_inner = jnp.sum(soft_weights * grad_weights, -1, keepdims=True)
        grad_scores = (soft_weights * (grad_weights - row_inner)).astype(jnp.bfloat16)
        grad_queries = (
            jnp.einsum("hqk,khd->qhd", grad_scores, key_part, preferred_element_type=jnp.float32)
            * score_scale
        )
        grad_keys = (
            jnp.einsum("hqk,qhd->khd", grad_scores, query_part, preferred_element_type=jnp.float32)
            * score_scale
        )
        return (grad_queries, grad_keys, grad_values)

    query_grad_blocks, key_grad_items, value_grad_items = lax.map(
        attend_back,
        (
            query_blocks,
            grad_mixed.reshape(item_count, block_rows, HEADS, HEAD_DIM),
            log_sums,
            item_ids,
        ),
    )
    grad_queries = query_grad_blocks.reshape(total_rows, model_width).astype(jnp.bfloat16)
    grad_keys = key_grad_items.reshape(seq_count, seq_blocks, slot_count, model_width).sum(1)
    grad_keys = grad_keys.reshape(total_rows, model_width).astype(jnp.bfloat16)
    grad_values = value_grad_items.reshape(seq_count, seq_blocks, slot_count, model_width).sum(1)
    grad_values = grad_values.reshape(total_rows, model_width).astype(jnp.bfloat16)
    query_bias_grad = jnp.sum(grad_queries.astype(jnp.float32), 0)
    value_bias_grad = jnp.sum(grad_values.astype(jnp.float32), 0)
    query_weight_grad = outer_sum(flat_rows, grad_queries)
    key_weight_grad = outer_sum(flat_rows, grad_keys)
    value_weight_grad = outer_sum(flat_rows, grad_values)
    input_rows = (
        grad_h1
        + back_project(grad_queries, back_query)
        + back_project(grad_keys, back_key)
        + back_project(grad_values, back_value)
    )
    input_grad = input_rows.astype(jnp.bfloat16).reshape(seq_count, slot_count, model_width)
    owned = (
        lax.psum_scatter(
            query_weight_grad.astype(jnp.bfloat16), "group", scatter_dimension=0, tiled=True
        ).astype(jnp.float32),
        lax.psum_scatter(
            key_weight_grad.astype(jnp.bfloat16), "group", scatter_dimension=0, tiled=True
        ).astype(jnp.float32),
        lax.psum_scatter(
            value_weight_grad.astype(jnp.bfloat16), "group", scatter_dimension=0, tiled=True
        ).astype(jnp.float32),
        lax.psum_scatter(
            out_weight_grad.astype(jnp.bfloat16), "group", scatter_dimension=0, tiled=True
        ).astype(jnp.float32),
        lax.psum_scatter(
            in_weight_grad.astype(jnp.bfloat16), "group", scatter_dimension=0, tiled=True
        ).astype(jnp.float32),
        lax.psum_scatter(
            back_weight_grad.astype(jnp.bfloat16), "group", scatter_dimension=0, tiled=True
        ).astype(jnp.float32),
        lax.psum_scatter(
            query_bias_grad.astype(jnp.bfloat16), "group", scatter_dimension=0, tiled=True
        ).astype(jnp.float32),
        lax.psum_scatter(
            value_bias_grad.astype(jnp.bfloat16), "group", scatter_dimension=0, tiled=True
        ).astype(jnp.float32),
        lax.psum_scatter(
            out_bias_grad.astype(jnp.bfloat16), "group", scatter_dimension=0, tiled=True
        ).astype(jnp.float32),
        lax.psum_scatter(
            in_bias_grad.astype(jnp.bfloat16), "group", scatter_dimension=0, tiled=True
        ).astype(jnp.float32),
        lax.psum_scatter(
            back_bias_grad.astype(jnp.bfloat16), "group", scatter_dimension=0, tiled=True
        ).astype(jnp.float32),
        lax.psum_scatter(
            first_gain_grad.astype(jnp.bfloat16), "group", scatter_dimension=0, tiled=True
        ).astype(jnp.float32),
        lax.psum_scatter(
            first_shift_grad.astype(jnp.bfloat16), "group", scatter_dimension=0, tiled=True
        ).astype(jnp.float32),
        lax.psum_scatter(
            second_gain_grad.astype(jnp.bfloat16), "group", scatter_dimension=0, tiled=True
        ).astype(jnp.float32),
        lax.psum_scatter(
            second_shift_grad.astype(jnp.bfloat16), "group", scatter_dimension=0, tiled=True
        ).astype(jnp.float32),
    )
    summed = tuple(
        jax.tree.map(
            lambda part: part.astype(jnp.float32), lax.psum(for_sending(tuple(owned)), "replica")
        )
    )
    return (layer_out, input_grad) + summed


def solution(mesh):
    return jax.shard_map(
        per_device,
        mesh=mesh,
        in_specs=(
            P(("group", "replica"), None, None),
            P(("group", "replica"), None, None),
            P(("group", "replica")),
            P("group", None),
            P("group", None),
            P("group", None),
            P("group", None),
            P("group", None),
            P("group", None),
            P("group"),
            P("group"),
            P("group"),
            P("group"),
            P("group"),
            P("group"),
            P("group"),
            P("group"),
            P("group"),
        ),
        out_specs=(
            P(("group", "replica"), None, None),
            P(("group", "replica"), None, None),
            P("group", None),
            P("group", None),
            P("group", None),
            P("group", None),
            P("group", None),
            P("group", None),
            P("group"),
            P("group"),
            P("group"),
            P("group"),
            P("group"),
            P("group"),
            P("group"),
            P("group"),
            P("group"),
        ),
        check_vma=False,
    )
```

profile of v0, /device:TPU:0, one launch (start us, length us, event | category | flops | bytes accessed | tf_op | source)
XLA Modules:
  0.0 681.8 jit_solution(8906284838521225156)
XLA Ops:
  19.8 25.9 %all-reduce.18 = (bf16[768]{0:T(1024)(128)(2,1)S(1)}, bf16[768]{0:T(1024)(128)(2,1)S(1)}, bf16[768]{0:T(1024)(128)(2,1)S(1)}, bf16[768]{0:T(1024)(128)(2,1)S(1)}...) all-reduce(bf16[768]{0:T(1024)(128)(2,1)S(1)} %dynamic-update-slice, ...), channel_id=1, replica_groups=mesh['group'=8,'replica'=4] {'group'}, use_global_device_ids=true, to_apply=%add.1 | all-reduce | flops 5376 | bytes 21504
  51.0 7.9 %all-gather = bf16[8,1,384]{2,1,0:T(2,128)(2,1)S(1)} all-gather(bf16[1,1,384]{2,1,0:T(2,128)(2,1)S(1)} %reshape.248), channel_id=1, replica_groups=mesh['group'=8,'replica'=4] {'group'}, dimensions={0}, use_global_device_ids=true | all-gather | bytes 6912 | tf_op jit(solution)/shard_map/all_gather | solution.py:83
  70.7 17.6 %all-gather.12.cloned.1.call-done = bf16[768,768]{1,0:T(8,128)(2,1)} async-done(((bf16[96,768]{1,0:T(8,128)(2,1)}), bf16[768,768]{1,0:T(8,128)(2,1)}) %all-gather.12.cloned.1.call-update) | async-done | bytes 1179664 | tf_op jit(solution)/shard_map/all_gather | solution.py:75
  88.4 4.3 convolution_convert_fusion.3
  98.6 25.4 %while.30 = (s32[]{:T(128)}, bf16[2,512,12,64]{1,3,2,0:T(8,128)(2,1)}, f32[2,12,512]{2,1,0:T(8,128)S(1)}, s32[2]{0:T(128)S(1)}, bf16[2,512,12,64]{1,3,2,0:T(8,12...) while((s32[]{:T(128)}, ...), condition=%wide.region_3.4_spmd, body=%wide.region_0.3_spmd.sunk | while | flops 843442176 | bytes 47426260 | solution.py:155
  134.7 19.9 %all-gather.16.cloned.1.call-done = bf16[768,3072]{1,0:T(8,128)(2,1)} async-done(((bf16[96,3072]{1,0:T(8,128)(2,1)}), bf16[768,3072]{1,0:T(8,128)(2,1)}) %all-gather.16.cloned.1.call-update) | async-done | bytes 4718608 | tf_op jit(solution)/shard_map/all_gather | solution.py:78
  154.6 37.4 %fusion.48 = (bf16[1024,3072]{1,0:T(8,128)(2,1)}, f32[1024,3072]{1,0:T(8,128)}) fusion(f32[3072]{0:T(1024)S(1)} %bitcast.208, bf16[768,3072]{1,0:T(8,128)(2,1)} %all-gather.16.cloned.1.call-done, f32[1024,768]{1,0:T(8,128)} %copy-done.6, f32[768]{0:T(1024)S(1)} %convert_element_type.280, f32[768]{0:T(1024)S(1)} %convert_element_type.279, ...), kind=kOutput, calls=%fused_computation.60 | convolution fusion | flops 5043388416 | bytes 26765312 | tf_op jit(solution)/shard_map/dot_general | solution.py:19
  195.2 9.3 %fusion.78 = (f32[1024]{0:T(1024)S(1)}, f32[1024,768]{1,0:T(8,128)S(1)}) fusion(f32[768]{0:T(1024)S(1)} %copy-done.51, bf16[1024,3072]{1,0:T(8,128)(2,1)} %get-tuple-element.468, bf16[3072,768]{1,0:T(8,128)(2,1)} %all-gather.18.cloned.1.call-done, f32[768]{0:T(1024)S(1)} %convert_element_type.280, f32[768]{0:T(1024)S(1)} %convert_element_type.279, ...), kind=kOutput, calls=%fused_computation.138 | convolution fusion | flops 4837342208 | bytes 17323008 | tf_op jit(solution)/shard_map/dot_general | solution.py:19
  211.3 13.4 %fusion.79 = (bf16[3072]{0:T(1024)(128)(2,1)}, bf16[1024,3072]{1,0:T(8,128)(2,1)S(1)}) fusion(f32[1024,3072]{1,0:T(8,128)} %get-tuple-element.469, f32[3072]{0:T(1024)S(1)} %bitcast.209, bf16[3072,768]{1,0:T(8,128)(2,1)S(1)} %copy-done.54, f32[1024,768]{1,0:T(8,128)S(1)} %get-tuple-element.454), kind=kOutput, calls=%fused_computation.139 | convolution fusion | flops 4870370304 | bytes 26757120 | tf_op jit(solution)/shard_map/re,de->rd/dot_general | solution.py:27
  224.8 6.6 multiply_reduce_fusion.2
  246.9 53.8 %while.31 = (s32[]{:T(128)}, bf16[2,512,12,64]{1,3,2,0:T(8,128)(2,1)}, bf16[2,512,12,64]{1,3,2,0:T(8,128)(2,1)}, bf16[2,512,12,64]{1,3,2,0:T(8,128)(2,1)}, s32[2...) while((s32[]{:T(128)}, ...), condition=%wide.region_14.15_spmd, body=%wide.region_12.14_spmd.sunk | while | flops 2061232128 | bytes 155120608 | solution.py:250
  254.9 7.3 %multiply_reduce_fusion.10 = (f32[12,512]{1,0:T(8,128)S(1)}, f32[12,512,512]{1,2,0:T(8,128)}) fusion(f32[12,512,512]{1,2,0:T(8,128)S(1)} %fusion.139, f32[12,512]{1,0:T(8,128)S(1)} %dynamic-slice_bitcast_fusion.2, pred[512]{0:T(512)(128)(4,1)S(1)} %dynamic-slice_reduce_fusion.5, bf16[2,512,12,64]{1,3,2,0:T(8,128)(2,1)S(1)} %copy-done.3, ...), kind=kOutput, calls=%fused_computation.23.clone.1 | convolution fusion | flops 418375680 | bytes 26796552 | tf_op jit(solution)/shard_map/while/body/eval_jaxpr/qhd,khd->hqk/dot_general | solution.py:229
  262.2 7.2 %multiply_convert_fusion.2 = bf16[12,512,512]{1,2,0:T(8,128)(2,1)S(1)} fusion(f32[12,512,512]{1,2,0:T(8,128)} %get-tuple-element.599, f32[12,512,512]{1,2,0:T(8,128)S(1)} %fusion.139, f32[12,512]{1,0:T(8,128)S(1)} %get-tuple-element.600, f32[12,512]{1,0:T(8,128)S(1)} %dynamic-slice_bitcast_fusion.2, pred[512]{0:T(512)(128)(4,1)S(1)} %dynamic-slice_reduce_fusion.5), kind=kLoop, calls=%fused_computation.22.clone.1 | loop fusion | flops 18874368 | bytes 31506944 | tf_op jit(solution)/shard_map/while/body/eval_jaxpr/convert_element_type | solution.py:239
  281.6 7.3 %multiply_reduce_fusion.10 = (f32[12,512]{1,0:T(8,128)S(1)}, f32[12,512,512]{1,2,0:T(8,128)}) fusion(f32[12,512,512]{1,2,0:T(8,128)S(1)} %fusion.139, f32[12,512]{1,0:T(8,128)S(1)} %dynamic-slice_bitcast_fusion.2, pred[512]{0:T(512)(128)(4,1)S(1)} %dynamic-slice_reduce_fusion.5, bf16[2,512,12,64]{1,3,2,0:T(8,128)(2,1)S(1)} %copy-done.3, ...), kind=kOutput, calls=%fused_computation.23.clone.1 | convolution fusion | flops 418375680 | bytes 26796552 | tf_op jit(solution)/shard_map/while/body/eval_jaxpr/qhd,khd->hqk/dot_general | solution.py:229
  288.9 7.2 %multiply_convert_fusion.2 = bf16[12,512,512]{1,2,0:T(8,128)(2,1)S(1)} fusion(f32[12,512,512]{1,2,0:T(8,128)} %get-tuple-element.599, f32[12,512,512]{1,2,0:T(8,128)S(1)} %fusion.139, f32[12,512]{1,0:T(8,128)S(1)} %get-tuple-element.600, f32[12,512]{1,0:T(8,128)S(1)} %dynamic-slice_bitcast_fusion.2, pred[512]{0:T(512)(128)(4,1)S(1)} %dynamic-slice_reduce_fusion.5), kind=kLoop, calls=%fused_computation.22.clone.1 | loop fusion | flops 18874368 | bytes 31506944 | tf_op jit(solution)/shard_map/while/body/eval_jaxpr/convert_element_type | solution.py:239
  327.1 9.9 %convolution_convert_fusion = bf16[3072,768]{1,0:T(8,128)(2,1)} fusion(bf16[1024,3072]{1,0:T(8,128)(2,1)} %get-tuple-element.468, f32[1024,768]{1,0:T(8,128)} %copy-done.19), kind=kOutput, calls=%fused_computation.82 | convolution fusion | flops 4834983936 | bytes 14155776 | tf_op jit(solution)/shard_map/rd,re->de/dot_general | solution.py:23
  338.9 10.0 %convolution_convert_fusion.1 = bf16[768,3072]{1,0:T(8,128)(2,1)} fusion(bf16[1024,3072]{1,0:T(8,128)(2,1)} %copy-done.63, f32[1024,768]{1,0:T(8,128)S(1)} %copy-done.8, f32[768]{0:T(1024)S(1)} %copy-done.50, f32[768]{0:T(1024)S(1)} %copy-done.40, f32[1024]{0:T(1024)S(1)} %copy-done.42, f32[1024]{0:T(1024)S(1)} %copy-done.37), kind=kOutput, calls=%fused_computation.83 | convolution fusion | flops 4838129664 | bytes 14170112 | tf_op jit(solution)/shard_map/rd,re->de/dot_general | solution.py:23
  354.6 23.1 %all-reduce.17 = (bf16[768]{0:T(1024)(128)(2,1)S(1)}, bf16[768]{0:T(1024)(128)(2,1)S(1)}, bf16[768]{0:T(1024)(128)(2,1)S(1)}, bf16[768]{0:T(1024)(128)(2,1)S(1)}...) all-reduce(bf16[768]{0:T(1024)(128)(2,1)S(1)} %dynamic-update-slice, ...), channel_id=1, replica_groups=mesh['group'=8,'replica'=4] {'group'}, use_global_device_ids=true, to_apply=%add.7 | all-reduce | flops 9984 | bytes 39936
  378.4 11.8 %all-reduce.19 = (bf16[96]{0:T(256)(128)(2,1)S(1)}, bf16[96]{0:T(256)(128)(2,1)S(1)}, bf16[96]{0:T(256)(128)(2,1)S(1)}, bf16[384]{0:T(512)(128)(2,1)S(1)}, bf16[...) all-reduce(bf16[96]{0:T(256)(128)(2,1)S(1)} %dynamic-slice.9, ...), channel_id=1, replica_groups=mesh['group'=8,'replica'=4] {'replica'}, use_global_device_ids=true, to_apply=%region_29.30 | all-reduce | flops 1152 | bytes 4608 | tf_op jit(solution)/shard_map/psum | solution.py:325
  398.3 27.5 %reduce-scatter.21.cloned.1.call-done = bf16[96,768]{1,0:T(8,128)(2,1)} async-done(((bf16[768,768]{1,0:T(8,128)(2,1)}), bf16[96,768]{1,0:T(8,128)(2,1)}) %reduce-scatter.21.cloned.1.call-update) | async-done | bytes 147472
  427.5 38.6 %reduce-scatter.13.cloned.1.call-done = bf16[96,768]{1,0:T(8,128)(2,1)} async-done(((bf16[768,768]{1,0:T(8,128)(2,1)}), bf16[96,768]{1,0:T(8,128)(2,1)}) %reduce-scatter.13.cloned.1.call-update) | async-done | bytes 147472 | tf_op jit(solution)/shard_map/reduce_scatter | solution.py:286
  466.2 57.3 %reduce-scatter.17.cloned.1.call-done = bf16[384,768]{1,0:T(8,128)(2,1)} async-done(((bf16[3072,768]{1,0:T(8,128)(2,1)}), bf16[384,768]{1,0:T(8,128)(2,1)}) %reduce-scatter.17.cloned.1.call-update) | async-done | bytes 589840 | tf_op jit(solution)/shard_map/reduce_scatter | solution.py:292
  523.4 57.1 %reduce-scatter.15.cloned.1.call-done = bf16[96,3072]{1,0:T(8,128)(2,1)} async-done(((bf16[768,3072]{1,0:T(8,128)(2,1)}), bf16[96,3072]{1,0:T(8,128)(2,1)}) %reduce-scatter.15.cloned.1.call-update) | async-done | bytes 589840 | tf_op jit(solution)/shard_map/reduce_scatter | solution.py:289
  590.1 74.7 %all-reduce.23.cloned.1.call-done = (bf16[96,768]{0,1:T(8,128)(2,1)}, bf16[96,768]{0,1:T(8,128)(2,1)}, bf16[96,768]{0,1:T(8,128)(2,1)}, bf16[96,768]{1,0:T(8,128...) async-done(((bf16[96,768]{0,1:T(8,128)(2,1)}, bf16[96,768]{0,1:T(8,128)(2,1)}, bf16[96,768]{0,1:T(8,128)(2,1)}, bf16[96,768]{1,0:T(8,128)(2,1)}, ...) | async-done | bytes 1769488 | tf_op jit(solution)/shard_map/psum | solution.py:325
  (325 shorter events, 174.2 us)
Async XLA Ops:
  7.2 51.7 %all-gather.8.cloned.1.call-start = ((), (), s32[]{:S(2)}) async-start(), calls=%async_computation.6 | async-start | bytes 1327104 | tf_op jit(solution)/shard_map/all_gather | solution.py:76
  7.9 57.6 %all-gather.10.cloned.1.call-start = ((), (), s32[]{:S(2)}) async-start(), calls=%async_computation.7 | async-start | bytes 1327104 | tf_op jit(solution)/shard_map/all_gather | solution.py:74
  8.7 79.7 %all-gather.12.cloned.1.call-start = ((), (), s32[]{:S(2)}) async-start(), calls=%async_computation.8 | async-start | bytes 1327104 | tf_op jit(solution)/shard_map/all_gather | solution.py:75
  9.4 119.2 %all-gather.14.cloned.1.call-start = ((), (), s32[]{:S(2)}) async-start(), calls=%async_computation.9 | async-start | bytes 1327104 | tf_op jit(solution)/shard_map/all_gather | solution.py:77
  10.0 144.6 %all-gather.16.cloned.1.call-start = ((), (), s32[]{:S(2)}) async-start(), calls=%async_computation.10 | async-start | bytes 5308416 | tf_op jit(solution)/shard_map/all_gather | solution.py:78
  10.6 184.6 %all-gather.18.cloned.1.call-start = ((), (), s32[]{:S(2)}) async-start(), calls=%async_computation.11 | async-start | bytes 5308416 | tf_op jit(solution)/shard_map/all_gather | solution.py:79
  11.1 383.7 %reduce-scatter.19.cloned.1.call-start = ((), (), s32[]{:S(2)}) async-start(), calls=%async_computation.15 | async-start | bytes 1327104
  45.7 185.7 %copy-start.39 = (f32[768]{0:T(1024)}, f32[768]{0:T(1024)S(1)}, u32[]{:S(2)}) copy-start(f32[768]{0:T(1024)S(1)} %convert_element_type.279) | copy-start | bytes 9220
  45.7 149.5 %copy-start.49 = (f32[768]{0:T(1024)}, f32[768]{0:T(1024)S(1)}, u32[]{:S(2)}) copy-start(f32[768]{0:T(1024)S(1)} %convert_element_type.280) | copy-start | bytes 9220
  132.6 98.8 %copy-start.36 = (f32[1024]{0:T(1024)}, f32[1024]{0:T(1024)S(1)}, u32[]{:S(2)}) copy-start(f32[1024]{0:T(1024)S(1)} %broadcast_multiply_fusion.4) | copy-start | bytes 12292
  134.7 96.7 %copy-start.41 = (f32[1024]{0:T(1024)}, f32[1024]{0:T(1024)S(1)}, u32[]{:S(2)}) copy-start(f32[1024]{0:T(1024)S(1)} %add_rsqrt_fusion.1) | copy-start | bytes 12292
  154.6 40.6 %copy-start.51 = (f32[768]{0:T(1024)S(1)}, f32[768]{0:T(1024)}, u32[]{:S(2)}) copy-start(f32[768]{0:T(1024)} %convert_element_type.284) | copy-start | bytes 9220
  209.2 15.6 %slice-start = ((s8[4718592]{0:T(1024)(128)(4,1)}), s8[4194304]{0:T(1024)(128)(4,1)S(1)}, s32[]{:S(2)}) async-start(s8[4718592]{0:T(1024)(128)(4,1)} %bitcast.210), calls=%async_computation.19 | async-start | bytes 8388608
  211.3 13.5 %slice-start.1 = ((s8[4718592]{0:T(1024)(128)(4,1)}), s8[524288]{0:T(1024)(128)(4,1)S(1)}, s32[]{:S(2)}) async-start(s8[4718592]{0:T(1024)(128)(4,1)} %bitcast.210), calls=%async_computation.20 | async-start | bytes 1048576
  308.4 88.2 %reduce-scatter.23.cloned.1.call-start = ((), (), s32[]{:S(2)}) async-start(), calls=%async_computation.17 | async-start | bytes 1327104
  314.8 111.0 %reduce-scatter.21.cloned.1.call-start = ((), (), s32[]{:S(2)}) async-start(), calls=%async_computation.16 | async-start | bytes 1327104
  323.1 143.0 %reduce-scatter.13.cloned.1.call-start = ((), (), s32[]{:S(2)}) async-start(), calls=%async_computation.12 | async-start | bytes 1327104 | tf_op jit(solution)/shard_map/reduce_scatter | solution.py:286
  327.0 196.4 %reduce-scatter.17.cloned.1.call-start = ((), (), s32[]{:S(2)}) async-start(), calls=%async_computation.14 | async-start | bytes 5308416 | tf_op jit(solution)/shard_map/reduce_scatter | solution.py:292
  337.0 243.5 %reduce-scatter.15.cloned.1.call-start = ((), (), s32[]{:S(2)}) async-start(), calls=%async_computation.13 | async-start | bytes 5308416 | tf_op jit(solution)/shard_map/reduce_scatter | solution.py:289
  349.0 231.6 %copy-start.1 = (f32[1024,768]{1,0:T(8,128)S(1)}, f32[1024,768]{1,0:T(8,128)}, u32[]{:S(2)}) copy-start(f32[1024,768]{1,0:T(8,128)} %copy-done) | copy-start | bytes 9437188
  349.0 231.6 %copy-start.31 = (f32[768]{0:T(1024)S(1)}, f32[768]{0:T(1024)}, u32[]{:S(2)}) copy-start(f32[768]{0:T(1024)} %copy-done.29) | copy-start | bytes 9220
  349.0 231.6 %copy-start.33 = (f32[1024]{0:T(1024)S(1)}, f32[1024]{0:T(1024)}, u32[]{:S(2)}) copy-start(f32[1024]{0:T(1024)} %copy-done.32) | copy-start | bytes 12292
  349.0 231.6 %copy-start.35 = (f32[1024]{0:T(1024)S(1)}, f32[1024]{0:T(1024)}, u32[]{:S(2)}) copy-start(f32[1024]{0:T(1024)} %copy-done.34) | copy-start | bytes 12292
  349.0 315.8 %all-reduce.23.cloned.1.call-start = ((), (), s32[]{:S(2)}) async-start(), calls=%async_computation.18 | async-start | bytes 3833856 | tf_op jit(solution)/shard_map/psum | solution.py:325
  (64 other events, 226.8 us)
Sparse Core Ops, SparseCore 0:
  9.9 26.7 all-gather.7
  38.5 23.9 all-gather.9
  64.4 23.9 all-gather.11
  90.1 23.9 all-gather.13
  115.8 38.7 all-gather.15
  156.3 38.7 all-gather.17
  308.5 36.6 reduce-scatter.18
  348.4 36.8 reduce-scatter.22
  389.1 36.6 reduce-scatter.20
  429.4 36.6 reduce-scatter.12
  469.6 53.7 reduce-scatter.16
  526.7 53.7 reduce-scatter.14
  583.9 80.8 all-reduce.22
where the time goes:
time: 690 us; the launch traced here: 682 us
  waiting for transfers between devices  300 us (43%)
  matrix products  163 us (24%)
  local copies, waits for them, and re-layouts  77.7 us (11%)
  blocking collectives  68.7 us (10%)
  other arithmetic  45.5 us (7%)
  between operations  17.2 us (2%)
  loops' own time  8.97 us (1%)
    psum x1, waiting for transfers between devices, per_device(): lax.psum(for_sending(tuple(owned)), 'replica')  74.7 us
    dot_general x6, matrix products, project(): return jnp.dot(left, right, preferred_element_type=jnp.float32)  60.8 us
    reduce_scatter x1, waiting for transfers between devices, per_device(): lax.psum_scatter(back_weight_grad.astype(jnp.bfloat16), 'group', scatter_...  57.3 us
    reduce_scatter x1, waiting for transfers between devices, per_device(): lax.psum_scatter(in_weight_grad.astype(jnp.bfloat16), 'group', scatter_di...  57.1 us
    unnamed x2, blocking collectives  49 us
    unnamed x156, local copies, waits for them, and re-layouts  41.7 us
    reduce_scatter x1, waiting for transfers between devices, per_device(): lax.psum_scatter(out_weight_grad.astype(jnp.bfloat16), 'group', scatter_d...  38.6 us
    unnamed x16, waiting for transfers between devices  31.2 us
  transfers between devices with their start and end apart: 13, of which 8 were waited for; matrix products, arithmetic and copies ran while one was open for 23% of the time, Pallas kernels for 0%

commit v1 on v0

--- a/solution.py
+++ b/solution.py
@@ -9,6 +9,28 @@
 NORM_EPS = 1e-12
 inverse_root_two = 0.7071067811865476
 inverse_root_tau = 0.3989422804014327
+
+
+def joined_along(blocks, dim):
+    blocks = jnp.moveaxis(blocks, 0, dim)
+    shape = blocks.shape
+    return blocks.reshape(*shape[:dim], shape[dim] * shape[dim + 1], *shape[dim + 2 :])
+
+
+def grow_blocks(array, axis):
+    length = lax.axis_size(axis)
+    pieces = array[None]
+    for level in range(length.bit_length() - 1):
+        distance = 1 << level
+        received = lax.ppermute(pieces, axis, [(i, i ^ distance) for i in range(length)])
+        both = jnp.stack([pieces, received])
+        upper = lax.axis_index(axis) >> level & 1
+        pieces = jnp.where(upper == 0, both, both[::-1]).reshape(-1, *array.shape)
+    return pieces
+
+
+def doubled_up(shard, axis, dim):
+    return joined_along(grow_blocks(shard, axis), dim)
 
 
 def for_sending(array):
@@ -72,7 +94,7 @@
 ):
     whole = (
         lax.all_gather(query_weight, "group", axis=0, tiled=True),
-        lax.all_gather(key_weight, "group", axis=0, tiled=True),
+        doubled_up(key_weight, "group", 0),
         lax.all_gather(value_weight, "group", axis=0, tiled=True),
         lax.all_gather(out_weight, "group", axis=0, tiled=True),
         lax.all_gather(in_weight, "group", axis=0, tiled=True),

time: 690 us -> 694 us (level)
  blocking collectives: 68.7 us -> 75.7 us
  waiting for transfers between devices: 300 us -> 293 us
    all_gather x1, waiting for transfers between devices: 19.9 us -> 7.26 us  [per_device(): lax.all_gather(in_weight, 'group', axis=0, tiled=True)]
    all_gather x1, blocking collectives: 7.91 us -> 15.4 us  [per_device(): lax.all_gather(in_bias, 'group', axis=0, tiled=True)]
    unnamed x156 -> x178, local copies, waits for them, and re-layouts: 41.7 us -> 34.5 us
  transfers between devices with their start and end apart: 13 -> 16, of which waited for: 8 -> 9; matrix products, arithmetic and copies ran while one was open for 23% -> 23% of each run, Pallas kernels for 0% -> 0%
where the time goes in v1:
time: 694 us; the launch traced here: 685 us
  waiting for transfers between devices  293 us (42%)
  matrix products  166 us (24%)
  blocking collectives  75.7 us (11%)
  local copies, waits for them, and re-layouts  73.3 us (11%)
  other arithmetic  44.8 us (6%)
  between operations  17.4 us (3%)
  loops' own time  8.97 us (1%)
    psum x1, waiting for transfers between devices, per_device(): lax.psum(for_sending(tuple(owned)), 'replica')  77.9 us
    dot_general x6, matrix products, project(): return jnp.dot(left, right, preferred_element_type=jnp.float32)  60.2 us
    reduce_scatter x1, waiting for transfers between devices, per_device(): lax.psum_scatter(in_weight_grad.astype(jnp.bfloat16), 'group', scatter_di...  57.2 us
    reduce_scatter x1, waiting for transfers between devices, per_device(): lax.psum_scatter(back_weight_grad.astype(jnp.bfloat16), 'group', scatter_...  57.1 us
    unnamed x2, blocking collectives  48.4 us
    reduce_scatter x1, waiting for transfers between devices, per_device(): lax.psum_scatter(out_weight_grad.astype(jnp.bfloat16), 'group', scatter_d...  38.8 us
    unnamed x178, local copies, waits for them, and re-layouts  34.5 us
    dot_general x6, matrix products, back_project(): jnp.einsum('re,de->rd', grad_rows, weight_full, preferred_element_type=jn...  31.9 us
  transfers between devices with their start and end apart: 16, of which 9 were waited for; matrix products, arithmetic and copies ran while one was open for 23% of the time, Pallas kernels for 0%

profile of v1, /device:TPU:0, one launch (start us, length us, event | category | flops | bytes accessed | tf_op | source)
XLA Modules:
  0.0 685.1 jit_solution(6678811101032192082)
XLA Ops:
  18.9 25.1 %all-reduce.18 = (bf16[768]{0:T(1024)(128)(2,1)S(1)}, bf16[768]{0:T(1024)(128)(2,1)S(1)}, bf16[768]{0:T(1024)(128)(2,1)S(1)}, bf16[768]{0:T(1024)(128)(2,1)S(1)}...) all-reduce(bf16[768]{0:T(1024)(128)(2,1)S(1)} %dynamic-update-slice, ...), channel_id=1, replica_groups=mesh['group'=8,'replica'=4] {'group'}, use_global_device_ids=true, to_apply=%add.1 | all-reduce | flops 5376 | bytes 21504
  49.0 15.4 %all-gather = bf16[8,1,384]{2,1,0:T(2,128)(2,1)S(1)} all-gather(bf16[1,1,384]{2,1,0:T(2,128)(2,1)S(1)} %reshape.256), channel_id=1, replica_groups=mesh['group'=8,'replica'=4] {'group'}, dimensions={0}, use_global_device_ids=true | all-gather | bytes 6912 | tf_op jit(solution)/shard_map/all_gather | solution.py:105
  67.8 4.3 add_convert_fusion.3
  88.7 25.4 %while.30 = (s32[]{:T(128)}, bf16[2,512,12,64]{1,3,2,0:T(8,128)(2,1)}, f32[2,12,512]{2,1,0:T(8,128)S(1)}, s32[2]{0:T(128)S(1)}, bf16[2,512,12,64]{1,3,2,0:T(8,12...) while((s32[]{:T(128)}, ...), condition=%wide.region_3.4_spmd, body=%wide.region_0.3_spmd.sunk | while | flops 843442176 | bytes 47426260 | solution.py:177
  124.9 7.3 %all-gather.14.cloned.1.call-done = bf16[768,3072]{1,0:T(8,128)(2,1)} async-done(((bf16[96,3072]{1,0:T(8,128)(2,1)}), bf16[768,3072]{1,0:T(8,128)(2,1)}) %all-gather.14.cloned.1.call-update) | async-done | bytes 4718608 | tf_op jit(solution)/shard_map/all_gather | solution.py:100
  132.1 37.4 %fusion.48 = (bf16[1024,3072]{1,0:T(8,128)(2,1)}, f32[1024,3072]{1,0:T(8,128)}) fusion(f32[3072]{0:T(1024)S(1)} %bitcast.230, bf16[768,3072]{1,0:T(8,128)(2,1)} %all-gather.14.cloned.1.call-done, f32[1024,768]{1,0:T(8,128)} %copy-done.7, f32[768]{0:T(1024)S(1)} %convert_element_type.284, f32[768]{0:T(1024)S(1)} %convert_element_type.283, ...), kind=kOutput, calls=%fused_computation.60 | convolution fusion | flops 5043388416 | bytes 26765312 | tf_op jit(solution)/shard_map/dot_general | solution.py:41
  172.7 9.3 %fusion.81 = (f32[1024]{0:T(1024)S(1)}, f32[1024,768]{1,0:T(8,128)S(1)}) fusion(f32[768]{0:T(1024)S(1)} %copy-done.52, bf16[1024,3072]{1,0:T(8,128)(2,1)} %get-tuple-element.470, bf16[3072,768]{1,0:T(8,128)(2,1)} %all-gather.16.cloned.1.call-done, f32[768]{0:T(1024)S(1)} %convert_element_type.284, f32[768]{0:T(1024)S(1)} %convert_element_type.283, ...), kind=kOutput, calls=%fused_computation.147 | convolution fusion | flops 4837342208 | bytes 17323008 | tf_op jit(solution)/shard_map/dot_general | solution.py:41
  188.9 13.5 %fusion.82 = (bf16[3072]{0:T(1024)(128)(2,1)}, bf16[1024,3072]{1,0:T(8,128)(2,1)S(1)}) fusion(f32[1024,3072]{1,0:T(8,128)} %get-tuple-element.471, f32[3072]{0:T(1024)S(1)} %bitcast.231, bf16[3072,768]{1,0:T(8,128)(2,1)S(1)} %copy-done.58, f32[1024,768]{1,0:T(8,128)S(1)} %get-tuple-element.454), kind=kOutput, calls=%fused_computation.148 | convolution fusion | flops 4870370304 | bytes 26757120 | tf_op jit(solution)/shard_map/re,de->rd/dot_general | solution.py:49
  202.3 6.6 multiply_reduce_fusion.2
  224.3 53.9 %while.31 = (s32[]{:T(128)}, bf16[2,512,12,64]{1,3,2,0:T(8,128)(2,1)}, bf16[2,512,12,64]{1,3,2,0:T(8,128)(2,1)}, bf16[2,512,12,64]{1,3,2,0:T(8,128)(2,1)}, s32[2...) while((s32[]{:T(128)}, ...), condition=%wide.region_14.15_spmd, body=%wide.region_12.14_spmd.sunk | while | flops 2061232128 | bytes 155120608 | solution.py:272
  232.3 7.3 %multiply_reduce_fusion.10 = (f32[12,512]{1,0:T(8,128)S(1)}, f32[12,512,512]{1,2,0:T(8,128)}) fusion(f32[12,512,512]{1,2,0:T(8,128)S(1)} %fusion.142, f32[12,512]{1,0:T(8,128)S(1)} %dynamic-slice_bitcast_fusion.2, pred[512]{0:T(512)(128)(4,1)S(1)} %dynamic-slice_reduce_fusion.5, bf16[2,512,12,64]{1,3,2,0:T(8,128)(2,1)S(1)} %copy-done.3, ...), kind=kOutput, calls=%fused_computation.23.clone.1 | convolution fusion | flops 418375680 | bytes 26796552 | tf_op jit(solution)/shard_map/while/body/eval_jaxpr/qhd,khd->hqk/dot_general | solution.py:251
  239.6 7.2 %multiply_convert_fusion.2 = bf16[12,512,512]{1,2,0:T(8,128)(2,1)S(1)} fusion(f32[12,512,512]{1,2,0:T(8,128)} %get-tuple-element.601, f32[12,512,512]{1,2,0:T(8,128)S(1)} %fusion.142, f32[12,512]{1,0:T(8,128)S(1)} %get-tuple-element.602, f32[12,512]{1,0:T(8,128)S(1)} %dynamic-slice_bitcast_fusion.2, pred[512]{0:T(512)(128)(4,1)S(1)} %dynamic-slice_reduce_fusion.5), kind=kLoop, calls=%fused_computation.22.clone.1 | loop fusion | flops 18874368 | bytes 31506944 | tf_op jit(solution)/shard_map/while/body/eval_jaxpr/convert_element_type | solution.py:261
  259.0 7.3 %multiply_reduce_fusion.10 = (f32[12,512]{1,0:T(8,128)S(1)}, f32[12,512,512]{1,2,0:T(8,128)}) fusion(f32[12,512,512]{1,2,0:T(8,128)S(1)} %fusion.142, f32[12,512]{1,0:T(8,128)S(1)} %dynamic-slice_bitcast_fusion.2, pred[512]{0:T(512)(128)(4,1)S(1)} %dynamic-slice_reduce_fusion.5, bf16[2,512,12,64]{1,3,2,0:T(8,128)(2,1)S(1)} %copy-done.3, ...), kind=kOutput, calls=%fused_computation.23.clone.1 | convolution fusion | flops 418375680 | bytes 26796552 | tf_op jit(solution)/shard_map/while/body/eval_jaxpr/qhd,khd->hqk/dot_general | solution.py:251
  266.3 7.2 %multiply_convert_fusion.2 = bf16[12,512,512]{1,2,0:T(8,128)(2,1)S(1)} fusion(f32[12,512,512]{1,2,0:T(8,128)} %get-tuple-element.601, f32[12,512,512]{1,2,0:T(8,128)S(1)} %fusion.142, f32[12,512]{1,0:T(8,128)S(1)} %get-tuple-element.602, f32[12,512]{1,0:T(8,128)S(1)} %dynamic-slice_bitcast_fusion.2, pred[512]{0:T(512)(128)(4,1)S(1)} %dynamic-slice_reduce_fusion.5), kind=kLoop, calls=%fused_computation.22.clone.1 | loop fusion | flops 18874368 | bytes 31506944 | tf_op jit(solution)/shard_map/while/body/eval_jaxpr/convert_element_type | solution.py:261
  304.6 9.9 %convolution_convert_fusion = bf16[3072,768]{1,0:T(8,128)(2,1)} fusion(bf16[1024,3072]{1,0:T(8,128)(2,1)} %get-tuple-element.470, f32[1024,768]{1,0:T(8,128)} %copy-done.20), kind=kOutput, calls=%fused_computation.82 | convolution fusion | flops 4834983936 | bytes 14155776 | tf_op jit(solution)/shard_map/rd,re->de/dot_general | solution.py:45
  316.3 10.0 %convolution_convert_fusion.1 = bf16[768,3072]{1,0:T(8,128)(2,1)} fusion(bf16[1024,3072]{1,0:T(8,128)(2,1)} %copy-done.74, f32[1024,768]{1,0:T(8,128)S(1)} %copy-done.9, f32[768]{0:T(1024)S(1)} %copy-done.51, f32[768]{0:T(1024)S(1)} %copy-done.41, f32[1024]{0:T(1024)S(1)} %copy-done.43, f32[1024]{0:T(1024)S(1)} %copy-done.38), kind=kOutput, calls=%fused_computation.83 | convolution fusion | flops 4838129664 | bytes 14170112 | tf_op jit(solution)/shard_map/rd,re->de/dot_general | solution.py:45
  332.6 23.3 %all-reduce.17 = (bf16[768]{0:T(1024)(128)(2,1)S(1)}, bf16[768]{0:T(1024)(128)(2,1)S(1)}, bf16[768]{0:T(1024)(128)(2,1)S(1)}, bf16[768]{0:T(1024)(128)(2,1)S(1)}...) all-reduce(bf16[768]{0:T(1024)(128)(2,1)S(1)} %dynamic-update-slice, ...), channel_id=1, replica_groups=mesh['group'=8,'replica'=4] {'group'}, use_global_device_ids=true, to_apply=%add.7 | all-reduce | flops 9984 | bytes 39936
  356.5 11.8 %all-reduce.19 = (bf16[96]{0:T(256)(128)(2,1)S(1)}, bf16[96]{0:T(256)(128)(2,1)S(1)}, bf16[96]{0:T(256)(128)(2,1)S(1)}, bf16[384]{0:T(512)(128)(2,1)S(1)}, bf16[...) all-reduce(bf16[96]{0:T(256)(128)(2,1)S(1)} %dynamic-slice.9, ...), channel_id=1, replica_groups=mesh['group'=8,'replica'=4] {'replica'}, use_global_device_ids=true, to_apply=%region_29.30 | all-reduce | flops 1152 | bytes 4608 | tf_op jit(solution)/shard_map/psum | solution.py:347
  376.5 26.7 %reduce-scatter.21.cloned.1.call-done = bf16[96,768]{1,0:T(8,128)(2,1)} async-done(((bf16[768,768]{1,0:T(8,128)(2,1)}), bf16[96,768]{1,0:T(8,128)(2,1)}) %reduce-scatter.21.cloned.1.call-update) | async-done | bytes 147472
  405.0 38.8 %reduce-scatter.13.cloned.1.call-done = bf16[96,768]{1,0:T(8,128)(2,1)} async-done(((bf16[768,768]{1,0:T(8,128)(2,1)}), bf16[96,768]{1,0:T(8,128)(2,1)}) %reduce-scatter.13.cloned.1.call-update) | async-done | bytes 147472 | tf_op jit(solution)/shard_map/reduce_scatter | solution.py:308
  443.7 57.1 %reduce-scatter.17.cloned.1.call-done = bf16[384,768]{1,0:T(8,128)(2,1)} async-done(((bf16[3072,768]{1,0:T(8,128)(2,1)}), bf16[384,768]{1,0:T(8,128)(2,1)}) %reduce-scatter.17.cloned.1.call-update) | async-done | bytes 589840 | tf_op jit(solution)/shard_map/reduce_scatter | solution.py:314
  500.8 57.2 %reduce-scatter.15.cloned.1.call-done = bf16[96,3072]{1,0:T(8,128)(2,1)} async-done(((bf16[768,3072]{1,0:T(8,128)(2,1)}), bf16[96,3072]{1,0:T(8,128)(2,1)}) %reduce-scatter.15.cloned.1.call-update) | async-done | bytes 589840 | tf_op jit(solution)/shard_map/reduce_scatter | solution.py:311
  563.5 20.2 %all-gather.18.cloned.1.call-done = bf16[768,768]{1,0:T(8,128)(2,1)} async-done(((bf16[96,768]{1,0:T(8,128)(2,1)}), bf16[768,768]{1,0:T(8,128)(2,1)}) %all-gather.18.cloned.1.call-update) | async-done | bytes 1179664 | tf_op jit(solution)/shard_map/all_gather | solution.py:195
  590.2 77.9 %all-reduce.23.cloned.1.call-done = (bf16[96,768]{0,1:T(8,128)(2,1)}, bf16[96,768]{0,1:T(8,128)(2,1)}, bf16[96,768]{0,1:T(8,128)(2,1)}, bf16[96,768]{1,0:T(8,128...) async-done(((bf16[96,768]{0,1:T(8,128)(2,1)}, bf16[96,768]{0,1:T(8,128)(2,1)}, bf16[96,768]{0,1:T(8,128)(2,1)}, bf16[96,768]{1,0:T(8,128)(2,1)}, ...) | async-done | bytes 1769488 | tf_op jit(solution)/shard_map/psum | solution.py:347
  (358 shorter events, 177.8 us)
Async XLA Ops:
  7.3 60.4 %all-gather.8.cloned.1.call-start = ((), (), s32[]{:S(2)}) async-start(), calls=%async_computation.6 | async-start | bytes 1327104 | tf_op jit(solution)/shard_map/all_gather | solution.py:98
  8.0 71.1 %all-gather.10.cloned.1.call-start = ((), (), s32[]{:S(2)}) async-start(), calls=%async_computation.7 | async-start | bytes 1327104 | tf_op jit(solution)/shard_map/all_gather | solution.py:96
  8.8 110.0 %all-gather.12.cloned.1.call-start = ((), (), s32[]{:S(2)}) async-start(), calls=%async_computation.8 | async-start | bytes 1327104 | tf_op jit(solution)/shard_map/all_gather | solution.py:99
  9.5 122.6 %all-gather.14.cloned.1.call-start = ((), (), s32[]{:S(2)}) async-start(), calls=%async_computation.9 | async-start | bytes 5308416 | tf_op jit(solution)/shard_map/all_gather | solution.py:100
  10.1 162.6 %all-gather.16.cloned.1.call-start = ((), (), s32[]{:S(2)}) async-start(), calls=%async_computation.10 | async-start | bytes 5308416 | tf_op jit(solution)/shard_map/all_gather | solution.py:101
  10.1 1.8 collective-permute-start
  12.9 31.8 %collective-permute-start.1 = (bf16[2,96,768]{2,1,0:T(8,128)(2,1)S(1)}, bf16[2,96,768]{2,1,0:T(8,128)(2,1)S(1)}, u32[]{:S(2)}, u32[]{:S(2)}) collective-permute-start(bf16[2,96,768]{2,1,0:T(8,128)(2,1)S(1)} %get-tuple-element.462), channel_id=1, source_target_pairs={{0,8},{4,12},{8,0},{12,4},{16,24},{20,28},{24,16},{28,20},{1,9},{5... | collective-permute-start | bytes 884744 | tf_op jit(solution)/shard_map/ppermute | solution.py:25
  15.9 357.2 %reduce-scatter.19.cloned.1.call-start = ((), (), s32[]{:S(2)}) async-start(), calls=%async_computation.15 | async-start | bytes 1327104
  44.1 164.8 %copy-start.40 = (f32[768]{0:T(1024)}, f32[768]{0:T(1024)S(1)}, u32[]{:S(2)}) copy-start(f32[768]{0:T(1024)S(1)} %convert_element_type.283) | copy-start | bytes 9220
  44.1 128.6 %copy-start.50 = (f32[768]{0:T(1024)}, f32[768]{0:T(1024)S(1)}, u32[]{:S(2)}) copy-start(f32[768]{0:T(1024)S(1)} %convert_element_type.284) | copy-start | bytes 9220
  44.9 19.5 %collective-permute-start.2 = (bf16[4,96,768]{2,1,0:T(8,128)(2,1)S(1)}, bf16[4,96,768]{2,1,0:T(8,128)(2,1)S(1)}, u32[]{:S(2)}, u32[]{:S(2)}) collective-permute-start(bf16[4,96,768]{2,1,0:T(8,128)(2,1)S(1)} %bitcast.211), channel_id=1, source_target_pairs={{0,16},{4,20},{8,24},{12,28},{16,0},{20,4},{24,8},{28,12},{1,17},{... | collective-permute-start | bytes 1769480 | tf_op jit(solution)/shard_map/ppermute | solution.py:25
  122.7 86.2 %copy-start.37 = (f32[1024]{0:T(1024)}, f32[1024]{0:T(1024)S(1)}, u32[]{:S(2)}) copy-start(f32[1024]{0:T(1024)S(1)} %broadcast_multiply_fusion.4) | copy-start | bytes 12292
  124.8 84.1 %copy-start.42 = (f32[1024]{0:T(1024)}, f32[1024]{0:T(1024)S(1)}, u32[]{:S(2)}) copy-start(f32[1024]{0:T(1024)S(1)} %add_rsqrt_fusion.1) | copy-start | bytes 12292
  285.8 89.0 %reduce-scatter.23.cloned.1.call-start = ((), (), s32[]{:S(2)}) async-start(), calls=%async_computation.17 | async-start | bytes 1327104
  292.2 111.0 %reduce-scatter.21.cloned.1.call-start = ((), (), s32[]{:S(2)}) async-start(), calls=%async_computation.16 | async-start | bytes 1327104
  300.6 143.1 %reduce-scatter.13.cloned.1.call-start = ((), (), s32[]{:S(2)}) async-start(), calls=%async_computation.12 | async-start | bytes 1327104 | tf_op jit(solution)/shard_map/reduce_scatter | solution.py:308
  304.5 196.3 %reduce-scatter.17.cloned.1.call-start = ((), (), s32[]{:S(2)}) async-start(), calls=%async_computation.14 | async-start | bytes 5308416 | tf_op jit(solution)/shard_map/reduce_scatter | solution.py:314
  314.5 243.6 %reduce-scatter.15.cloned.1.call-start = ((), (), s32[]{:S(2)}) async-start(), calls=%async_computation.13 | async-start | bytes 5308416 | tf_op jit(solution)/shard_map/reduce_scatter | solution.py:311
  326.5 257.3 %all-gather.18.cloned.1.call-start = ((), (), s32[]{:S(2)}) async-start(), calls=%async_computation.11 | async-start | bytes 1327104 | tf_op jit(solution)/shard_map/all_gather | solution.py:195
  327.0 231.0 %copy-start.1 = (f32[1024,768]{1,0:T(8,128)S(1)}, f32[1024,768]{1,0:T(8,128)}, u32[]{:S(2)}) copy-start(f32[1024,768]{1,0:T(8,128)} %copy-done) | copy-start | bytes 9437188
  327.0 231.0 %copy-start.32 = (f32[768]{0:T(1024)S(1)}, f32[768]{0:T(1024)}, u32[]{:S(2)}) copy-start(f32[768]{0:T(1024)} %copy-done.30) | copy-start | bytes 9220
  327.1 231.0 %copy-start.34 = (f32[1024]{0:T(1024)S(1)}, f32[1024]{0:T(1024)}, u32[]{:S(2)}) copy-start(f32[1024]{0:T(1024)} %copy-done.33) | copy-start | bytes 12292
  327.1 231.0 %copy-start.36 = (f32[1024]{0:T(1024)S(1)}, f32[1024]{0:T(1024)}, u32[]{:S(2)}) copy-start(f32[1024]{0:T(1024)} %copy-done.35) | copy-start | bytes 12292
  327.1 340.9 %all-reduce.23.cloned.1.call-start = ((), (), s32[]{:S(2)}) async-start(), calls=%async_computation.18 | async-start | bytes 3833856 | tf_op jit(solution)/shard_map/psum | solution.py:347
  (78 other events, 534.2 us)
Sparse Core Ops, SparseCore 0:
  10.0 28.1 all-gather.7
  40.1 25.5 all-gather.9
  67.6 23.9 all-gather.11
  93.3 38.7 all-gather.13
  133.8 38.7 all-gather.15
  285.9 36.6 reduce-scatter.18
  325.9 36.8 reduce-scatter.22
  366.5 36.6 reduce-scatter.20
  407.0 36.6 reduce-scatter.12
  447.0 53.7 reduce-scatter.16
  504.3 53.7 reduce-scatter.14
  559.8 23.9 all-gather.17
  587.2 80.7 all-reduce.22
